TPU v7x, 32 devices: a whole 2x2x4 slice. The times are simulated.
32 devices in a mesh: pipe: 4 (over x, core), tensor: 8 (over z, y).
Axes of the slice: x: 2, y: 2, z: 4, core: 2. Of those that a mesh axis runs over, the one named last changes fastest.
Arguments:
- hidden: bfloat16 [384, 8192], P('pipe', 'tensor'), may hold values from -64 to 64
- weight: bfloat16 [8192, 16384], P(None, ('pipe', 'tensor')), may hold values from -0.23201941 to 0.23201941
- targets: int32 [384], replicated, may hold values from 0 to 16383
- token_weight: float32 [384], replicated, may hold values from 0.1 to 1
Outputs:
- token_loss: float32 [384], P('pipe')
- hidden_grad: float32 [384, 8192], P('pipe', 'tensor')
All inputs are finite; a program needn't handle non-finite values.
Results may differ from a plain program's by a relative error of at most 0.0029.
Values may be sent and summed in bfloat16 or wider, within the bound.
A program may use at most 128 MiB of HBM per device.

v0:
```python
import jax
import jax.numpy as jnp
from jax import lax
from jax.sharding import PartitionSpec as P

loss_scale = 32.0


def local(hidden, weight, targets, token_weight):
    rows_local = hidden.shape[0]
    width_local = weight.shape[1]
    full_rows = lax.all_gather(hidden, "tensor", axis=1, tiled=True)
    logits = jnp.dot(
        lax.all_gather(full_rows, "pipe", axis=0, tiled=True),
        weight,
        preferred_element_type=jnp.float32,
    )
    device_block = lax.axis_index("pipe") * lax.axis_size("tensor") + lax.axis_index("tensor")
    columns = device_block * width_local + jnp.arange(width_local, dtype=jnp.int32)
    target_hit = targets[:, None] == columns[None, :]
    chosen = jnp.sum(jnp.where(target_hit, logits, jnp.float32(0.0)), axis=1)
    local_peak = jnp.max(logits, axis=1)
    global_peak = lax.pmax(local_peak, ("pipe", "tensor"))
    local_total = jnp.sum(jnp.exp(logits - global_peak[:, None]), axis=1)
    global_total, target_logit = lax.psum((local_total, chosen), ("pipe", "tensor"))
    log_total = global_peak + jnp.log(global_total)
    loss_rows = log_total - target_logit
    token_loss = lax.dynamic_slice_in_dim(
        loss_rows, lax.axis_index("pipe") * rows_local, rows_local, 0
    )
    softmax = jnp.exp(logits - log_total[:, None])
    dlogits = (
        loss_scale * token_weight[:, None] * (softmax - target_hit.astype(jnp.float32))
    ).astype(jnp.bfloat16)
    section_part = lax.psum_scatter(
        lax.dot_general(
            dlogits, weight, (((1,), (1,)), ((), ())), preferred_element_type=jnp.float32
        ),
        "pipe",
        scatter_dimension=0,
        tiled=True,
    )
    hidden_grad = lax.psum_scatter(section_part, "tensor", scatter_dimension=1, tiled=True)
    return (token_loss, hidden_grad)


def solution(mesh):
    in_specs = (P("pipe", "tensor"), P(None, ("pipe", "tensor")), P(), P())
    out_specs = (P("pipe"), P("pipe", "tensor"))
    return jax.shard_map(local, mesh=mesh, in_specs=in_specs, out_specs=out_specs, check_vma=False)
```

profile of v0, /device:TPU:0, one launch (start us, length us, event | category | flops | bytes accessed | tf_op | source)
XLA Modules:
  0.0 389.2 jit_solution(3919256009394892303)
XLA Ops:
  7.2 0.0 all-gather.3.cloned.1.call-start
  7.2 0.7 all-gather.3.cloned.1.call-update
  7.9 0.0 all-gather.5.cloned.1.call-start
  7.9 49.2 %all-gather.3.cloned.1.call-done = bf16[96,8192]{1,0:T(8,128)(2,1)} async-done(((bf16[96,1024]{1,0:T(8,128)(2,1)}), bf16[96,8192]{1,0:T(8,128)(2,1)}) %all-gather.3.cloned.1.call-update) | async-done | bytes 1572880 | tf_op jit(solution)/shard_map/all_gather | solution.py:12
  57.1 0.0 all-gather.5.cloned.1.call-update
  57.1 0.0 reduce-scatter.3.cloned.1.call-start
  57.2 0.7 broadcast_multiply_fusion
  57.9 0.0 copy-start
  57.9 45.5 %all-gather.5.cloned.1.call-done = bf16[384,8192]{1,0:T(8,128)(2,1)} async-done(((bf16[96,8192]{1,0:T(8,128)(2,1)}), bf16[384,8192]{1,0:T(8,128)(2,1)}) %all-gather.5.cloned.1.call-update) | async-done | bytes 6291472 | tf_op jit(solution)/shard_map/all_gather | solution.py:14
  103.4 8.0 %fusion.11 = (f32[384]{0:T(512)S(1)}, f32[384,512]{1,0:T(8,128)S(1)}) fusion(bf16[384,8192]{1,0:T(8,128)(2,1)} %all-gather.5.cloned.1.call-done, bf16[8192,512]{1,0:T(8,128)(2,1)} %param.5), kind=kOutput, calls=%fused_computation.16 | convolution fusion | flops 3221421568 | bytes 15468032 | tf_op jit(solution)/shard_map/dot_general | solution.py:13
  111.4 39.3 %pmax.7 = f32[384]{0:T(512)S(1)} all-reduce(f32[384]{0:T(512)S(1)} %get-tuple-element.8), channel_id=1, replica_groups=mesh['pipe'=4,'tensor'=8] {'pipe','tensor'}, use_global_device_ids=true, to_apply=%region_1.2 | all-reduce | flops 384 | bytes 3072 | tf_op jit(solution)/shard_map/pmax | solution.py:23
  150.7 0.0 copy-done
  150.7 0.3 fusion
  151.1 41.0 %all-reduce = (f32[384]{0:T(512)S(1)}, f32[384]{0:T(512)S(1)}) all-reduce(f32[384]{0:T(512)S(1)} %get-tuple-element.3, f32[384]{0:T(512)S(1)} %get-tuple-element.2), channel_id=1, replica_groups=mesh['pipe'=4,'tensor'=8] {'pipe','tensor'}, use_global_device_ids=true, to_apply=%region_3.4 | all-reduce | flops 768 | bytes 6144 | tf_op jit(solution)/shard_map/psum | solution.py:25
  192.1 12.0 %fusion.4 = f32[384,8192]{1,0:T(8,128)} fusion(bf16[8192,512]{1,0:T(8,128)(2,1)} %param.5, f32[384,512]{1,0:T(8,128)S(1)} %get-tuple-element.9, f32[384]{0:T(512)S(1)} %get-tuple-element.7, f32[384]{0:T(512)S(1)} %broadcast_multiply_fusion, s32[512]{0:T(512)S(1)} %iota_add_fusion, s32[384]{0:T(512)S(1)} %copy-done), kind=kOutput, calls=%fused_computation.7 | convolution fusion | flops 3222405120 | bytes 21764608 | tf_op jit(solution)/shard_map/dot_general | solution.py:36
  204.1 0.0 reduce-scatter.3.cloned.1.call-update
  204.1 0.0 reduce-scatter.5.cloned.1.call-start
  204.1 99.5 %reduce-scatter.3.cloned.1.call-done = f32[96,8192]{1,0:T(8,128)} async-done(((f32[384,8192]{1,0:T(8,128)}), f32[96,8192]{1,0:T(8,128)}) %reduce-scatter.3.cloned.1.call-update) | async-done | bytes 3145744 | tf_op jit(solution)/shard_map/reduce_scatter | solution.py:35
  303.6 0.0 reduce-scatter.5.cloned.1.call-update
  303.6 0.6 dynamic_slice.3
  304.2 78.4 %reduce-scatter.5.cloned.1.call-done = f32[96,1024]{1,0:T(8,128)} async-done(((f32[96,8192]{1,0:T(8,128)}), f32[96,1024]{1,0:T(8,128)}) %reduce-scatter.5.cloned.1.call-update) | async-done | bytes 393232 | tf_op jit(solution)/shard_map/reduce_scatter | solution.py:43
  (2 shorter events, 0.0 us)
Async XLA Ops:
  7.2 49.9 %all-gather.3.cloned.1.call-start = ((), (), s32[]{:S(2)}) async-start(), calls=%async_computation.2 | async-start | bytes 1769472 | tf_op jit(solution)/shard_map/all_gather | solution.py:12
  7.9 95.5 %all-gather.5.cloned.1.call-start = ((), (), s32[]{:S(2)}) async-start(), calls=%async_computation.3 | async-start | bytes 7864320 | tf_op jit(solution)/shard_map/all_gather | solution.py:14
  57.1 246.5 %reduce-scatter.3.cloned.1.call-start = ((), (), s32[]{:S(2)}) async-start(), calls=%async_computation.4 | async-start | bytes 15728640 | tf_op jit(solution)/shard_map/reduce_scatter | solution.py:35
  57.9 92.9 %copy-start = (s32[384]{0:T(512)S(1)}, s32[384]{0:T(512)}, u32[]{:S(2)}) copy-start(s32[384]{0:T(512)} %param.6) | copy-start | bytes 4612
  204.1 178.6 %reduce-scatter.5.cloned.1.call-start = ((), (), s32[]{:S(2)}) async-start(), calls=%async_computation.5 | async-start | bytes 3538944 | tf_op jit(solution)/shard_map/reduce_scatter | solution.py:43
Sparse Core Ops, SparseCore 0:
  10.2 46.9 all-gather.2
  58.7 44.7 all-gather.4
  204.2 99.3 reduce-scatter.2
  307.7 74.9 reduce-scatter.4
where the time goes:
time: 390 us; the launch traced here: 389 us
  waiting for transfers between devices  273 us (70%)
  blocking collectives  80.3 us (21%)
  matrix products  20 us (5%)
  between operations  13.8 us (4%)
    reduce_scatter x1, waiting for transfers between devices, local(): lax.psum_scatter(lax.dot_general(dlogits, weight, (((1,), (1,)), ((), ())...  99.5 us
    reduce_scatter x1, waiting for transfers between devices, local(): lax.psum_scatter(section_part, 'tensor', scatter_dimension=1, tiled=True)  78.4 us
    all_gather x1, waiting for transfers between devices, local(): full_rows = lax.all_gather(hidden, 'tensor', axis=1, tiled=True)  49.2 us
    all_gather x1, waiting for transfers between devices, local(): lax.all_gather(full_rows, 'pipe', axis=0, tiled=True)  45.5 us
    psum x1, blocking collectives, local(): lax.psum((local_total, chosen), ('pipe', 'tensor'))  41 us
    pmax x1, blocking collectives, local(): global_peak = lax.pmax(local_peak, ('pipe', 'tensor'))  39.3 us
    dot_general x1, matrix products, local(): lax.dot_general(dlogits, weight, (((1,), (1,)), ((), ())), preferred_elem...  12 us
    dot_general x1, matrix products, local(): jnp.dot(lax.all_gather(full_rows, 'pipe', axis=0, tiled=True), weight, pr...  8 us
  transfers between devices with their start and end apart: 4, of which 4 were waited for; matrix products, arithmetic and copies ran while one was open for 0% of the time, Pallas kernels for 0%

commit v1 on v0

--- a/solution.py
+++ b/solution.py
@@ -2,14 +2,28 @@
 import jax.numpy as jnp
 from jax import lax
 from jax.sharding import PartitionSpec as P
+from jax.lax import axis_index, axis_size, ppermute
 
 loss_scale = 32.0
 
 
 def local(hidden, weight, targets, token_weight):
+
+    def panel_finish(on_dim, matrix):
+        group_axis = "tensor"
+        lanes = axis_size(group_axis)
+        reached = [None] * lanes
+        crops = tuple(((p, (p + 1) % lanes) for p in range(lanes)))
+        reached[lanes - 1] = matrix
+        for w in range(lanes - 2, -1, -1):
+            reached[w] = ppermute(reached[w + 1], axis_name=group_axis, perm=crops)
+        kept_arr = jnp.concatenate(reached, axis=on_dim)
+        even = (axis_index(group_axis) + 1) * matrix.shape[on_dim]
+        return jnp.roll(kept_arr, even, axis=on_dim)
+
     rows_local = hidden.shape[0]
     width_local = weight.shape[1]
-    full_rows = lax.all_gather(hidden, "tensor", axis=1, tiled=True)
+    full_rows = panel_finish(1, hidden)
     logits = jnp.dot(
         lax.all_gather(full_rows, "pipe", axis=0, tiled=True),
         weight,

time: 390 us -> 403 us (1.033)
  waiting for transfers between devices: 273 us -> 282 us
    ppermute x0 -> x7, waiting for transfers between devices: none -> 59.6 us  [panel_finish(): reached[w] = ppermute(reached[w + 1], axis_name=group_axis, perm=crops)]
    all_gather x1 -> x0, waiting for transfers between devices: 49.2 us -> none  [local(): full_rows = lax.all_gather(hidden, 'tensor', axis=1, tiled=True)]
  transfers between devices with their start and end apart: 4 -> 10, of which waited for: 4 -> 10; matrix products, arithmetic and copies ran while one was open for 0% -> 0% of each run, Pallas kernels for 0% -> 0%
where the time goes in v1:
time: 403 us; the launch traced here: 402 us
  waiting for transfers between devices  282 us (70%)
  blocking collectives  80.3 us (20%)
  matrix products  20 us (5%)
  between operations  13.9 us (3%)
    reduce_scatter x1, waiting for transfers between devices, local(): lax.psum_scatter(lax.dot_general(dlogits, weight, (((1,), (1,)), ((), ())...  99.7 us
    reduce_scatter x1, waiting for transfers between devices, local(): lax.psum_scatter(section_part, 'tensor', scatter_dimension=1, tiled=True)  78.6 us
    ppermute x7, waiting for transfers between devices, panel_finish(): reached[w] = ppermute(reached[w + 1], axis_name=group_axis, perm=crops)  59.6 us
    all_gather x1, waiting for transfers between devices, local(): lax.all_gather(full_rows, 'pipe', axis=0, tiled=True)  43.7 us
    psum x1, blocking collectives, local(): lax.psum((local_total, chosen), ('pipe', 'tensor'))  41 us
    pmax x1, blocking collectives, local(): global_peak = lax.pmax(local_peak, ('pipe', 'tensor'))  39.3 us
    dot_general x1, matrix products, local(): lax.dot_general(dlogits, weight, (((1,), (1,)), ((), ())), preferred_elem...  12 us
  transfers between devices with their start and end apart: 10, of which 10 were waited for; matrix products, arithmetic and copies ran while one was open for 0% of the time, Pallas kernels for 0%

profile of v1, /device:TPU:0, one launch (start us, length us, event | category | flops | bytes accessed | tf_op | source)
XLA Modules:
  0.0 402.4 jit_solution(2642962131138157066)
XLA Ops:
  7.2 0.0 all-gather.2.cloned.1.call-start
  7.2 3.0 collective-permute-start
  10.3 8.2 %collective-permute-done = bf16[96,1024]{1,0:T(8,128)(2,1)S(1)} collective-permute-done((bf16[96,1024]{1,0:T(8,128)(2,1)}, bf16[96,1024]{1,0:T(8,128)(2,1)S(1)}, u32[]{:S(2)}, u32[]{:S(2)}) %collective-permute-start) | collective-permute-done | bytes 196640 | tf_op jit(solution)/shard_map/ppermute | solution.py:19
  18.4 8.8 %collective-permute-done.1 = bf16[96,1024]{1,0:T(8,128)(2,1)S(1)} collective-permute-done((bf16[96,1024]{1,0:T(8,128)(2,1)S(1)}, bf16[96,1024]{1,0:T(8,128)(2,1)S(1)}, u32[]{:S(2)}, u32[]{:S(2)}) %collective-permute-start.1) | collective-permute-done | bytes 196640 | tf_op jit(solution)/shard_map/ppermute | solution.py:19
  27.2 8.4 %collective-permute-done.2 = bf16[96,1024]{1,0:T(8,128)(2,1)S(1)} collective-permute-done((bf16[96,1024]{1,0:T(8,128)(2,1)S(1)}, bf16[96,1024]{1,0:T(8,128)(2,1)S(1)}, u32[]{:S(2)}, u32[]{:S(2)}) %collective-permute-start.2) | collective-permute-done | bytes 196640 | tf_op jit(solution)/shard_map/ppermute | solution.py:19
  35.6 8.4 %collective-permute-done.3 = bf16[96,1024]{1,0:T(8,128)(2,1)S(1)} collective-permute-done((bf16[96,1024]{1,0:T(8,128)(2,1)S(1)}, bf16[96,1024]{1,0:T(8,128)(2,1)S(1)}, u32[]{:S(2)}, u32[]{:S(2)}) %collective-permute-start.3) | collective-permute-done | bytes 196640 | tf_op jit(solution)/shard_map/ppermute | solution.py:19
  43.9 8.4 %collective-permute-done.4 = bf16[96,1024]{1,0:T(8,128)(2,1)S(1)} collective-permute-done((bf16[96,1024]{1,0:T(8,128)(2,1)S(1)}, bf16[96,1024]{1,0:T(8,128)(2,1)S(1)}, u32[]{:S(2)}, u32[]{:S(2)}) %collective-permute-start.4) | collective-permute-done | bytes 196640 | tf_op jit(solution)/shard_map/ppermute | solution.py:19
  52.3 9.3 %collective-permute-done.5 = bf16[96,1024]{1,0:T(8,128)(2,1)S(1)} collective-permute-done((bf16[96,1024]{1,0:T(8,128)(2,1)S(1)}, bf16[96,1024]{1,0:T(8,128)(2,1)S(1)}, u32[]{:S(2)}, u32[]{:S(2)}) %collective-permute-start.5) | collective-permute-done | bytes 196640 | tf_op jit(solution)/shard_map/ppermute | solution.py:19
  61.6 8.4 %collective-permute-done.6 = bf16[96,1024]{1,0:T(8,128)(2,1)S(1)} collective-permute-done((bf16[96,1024]{1,0:T(8,128)(2,1)S(1)}, bf16[96,1024]{1,0:T(8,128)(2,1)S(1)}, u32[]{:S(2)}, u32[]{:S(2)}) %collective-permute-start.6) | collective-permute-done | bytes 196640 | tf_op jit(solution)/shard_map/ppermute | solution.py:19
  70.1 0.9 constant_dynamic-update-slice_fusion.8
  71.2 1.3 constant_dynamic-slice_fusion
  72.5 0.0 all-gather.2.cloned.1.call-update
  72.5 0.0 reduce-scatter.3.cloned.1.call-start
  72.6 43.7 %all-gather.2.cloned.1.call-done = bf16[384,8192]{1,0:T(8,128)(2,1)} async-done(((bf16[96,8192]{1,0:T(8,128)(2,1)}), bf16[384,8192]{1,0:T(8,128)(2,1)}) %all-gather.2.cloned.1.call-update) | async-done | bytes 6291472 | tf_op jit(solution)/shard_map/all_gather | solution.py:28
  116.3 8.0 %fusion.11 = (f32[384]{0:T(512)S(1)}, f32[384,512]{1,0:T(8,128)S(1)}) fusion(bf16[384,8192]{1,0:T(8,128)(2,1)} %all-gather.2.cloned.1.call-done, bf16[8192,512]{1,0:T(8,128)(2,1)} %param.5), kind=kOutput, calls=%fused_computation.33 | convolution fusion | flops 3221421568 | bytes 15468032 | tf_op jit(solution)/shard_map/dot_general | solution.py:27
  124.3 39.3 %pmax.7 = f32[384]{0:T(512)S(1)} all-reduce(f32[384]{0:T(512)S(1)} %get-tuple-element.8), channel_id=1, replica_groups=mesh['pipe'=4,'tensor'=8] {'pipe','tensor'}, use_global_device_ids=true, to_apply=%region_1.2 | all-reduce | flops 384 | bytes 3072 | tf_op jit(solution)/shard_map/pmax | solution.py:37
  163.6 0.3 fusion
  164.0 41.0 %all-reduce = (f32[384]{0:T(512)S(1)}, f32[384]{0:T(512)S(1)}) all-reduce(f32[384]{0:T(512)S(1)} %get-tuple-element.3, f32[384]{0:T(512)S(1)} %get-tuple-element.2), channel_id=1, replica_groups=mesh['pipe'=4,'tensor'=8] {'pipe','tensor'}, use_global_device_ids=true, to_apply=%region_3.4 | all-reduce | flops 768 | bytes 6144 | tf_op jit(solution)/shard_map/psum | solution.py:39
  204.9 12.0 %fusion.4 = f32[384,8192]{1,0:T(8,128)} fusion(bf16[8192,512]{1,0:T(8,128)(2,1)} %param.5, f32[384,512]{1,0:T(8,128)S(1)} %get-tuple-element.9, f32[384]{0:T(512)S(1)} %get-tuple-element.7, f32[384]{0:T(512)S(1)} %broadcast_multiply_fusion, s32[512]{0:T(512)S(1)} %iota_add_fusion, s32[384]{0:T(512)S(1)} %copy-done.1), kind=kOutput, calls=%fused_computation.7 | convolution fusion | flops 3222405120 | bytes 21764608 | tf_op jit(solution)/shard_map/dot_general | solution.py:50
  216.9 0.0 reduce-scatter.5.cloned.1.call-start
  217.0 99.7 %reduce-scatter.3.cloned.1.call-done = f32[96,8192]{1,0:T(8,128)} async-done(((f32[384,8192]{1,0:T(8,128)}), f32[96,8192]{1,0:T(8,128)}) %reduce-scatter.3.cloned.1.call-update) | async-done | bytes 3145744 | tf_op jit(solution)/shard_map/reduce_scatter | solution.py:49
  316.7 0.0 reduce-scatter.5.cloned.1.call-update
  316.7 0.6 dynamic_slice.8
  317.3 78.6 %reduce-scatter.5.cloned.1.call-done = f32[96,1024]{1,0:T(8,128)} async-done(((f32[96,8192]{1,0:T(8,128)}), f32[96,1024]{1,0:T(8,128)}) %reduce-scatter.5.cloned.1.call-update) | async-done | bytes 393232 | tf_op jit(solution)/shard_map/reduce_scatter | solution.py:57
  (31 shorter events, 0.3 us)
Async XLA Ops:
  7.2 64.0 %copy-start = (bf16[96,1024]{1,0:T(8,128)(2,1)S(1)}, bf16[96,1024]{1,0:T(8,128)(2,1)}, u32[]{:S(2)}) copy-start(bf16[96,1024]{1,0:T(8,128)(2,1)} %param.4) | copy-start | bytes 589828
  7.2 109.1 %all-gather.2.cloned.1.call-start = ((), (), s32[]{:S(2)}) async-start(), calls=%async_computation.2 | async-start | bytes 7864320 | tf_op jit(solution)/shard_map/all_gather | solution.py:28
  7.2 11.2 %collective-permute-start = (bf16[96,1024]{1,0:T(8,128)(2,1)}, bf16[96,1024]{1,0:T(8,128)(2,1)S(1)}, u32[]{:S(2)}, u32[]{:S(2)}) collective-permute-start(bf16[96,1024]{1,0:T(8,128)(2,1)} %param.4), channel_id=1, source_target_pairs={{0,1},{1,2},{2,3},{3,4},{4,5},{5,6},{6,7},{7,0},{8,9},{9,10},{10,1... | collective-permute-start | bytes 589832 | tf_op jit(solution)/shard_map/ppermute | solution.py:19
  18.4 8.8 %collective-permute-start.1 = (bf16[96,1024]{1,0:T(8,128)(2,1)S(1)}, bf16[96,1024]{1,0:T(8,128)(2,1)S(1)}, u32[]{:S(2)}, u32[]{:S(2)}) collective-permute-start(bf16[96,1024]{1,0:T(8,128)(2,1)S(1)} %collective-permute-done), channel_id=1, source_target_pairs={{0,1},{1,2},{2,3},{3,4},{4,5},{5,6},{6,7},{7,0},{8,9},{9,10},{10,1... | collective-permute-start | bytes 589832 | tf_op jit(solution)/shard_map/ppermute | solution.py:19
  27.2 8.4 %collective-permute-start.2 = (bf16[96,1024]{1,0:T(8,128)(2,1)S(1)}, bf16[96,1024]{1,0:T(8,128)(2,1)S(1)}, u32[]{:S(2)}, u32[]{:S(2)}) collective-permute-start(bf16[96,1024]{1,0:T(8,128)(2,1)S(1)} %collective-permute-done.1), channel_id=1, source_target_pairs={{0,1},{1,2},{2,3},{3,4},{4,5},{5,6},{6,7},{7,0},{8,9},{9,10},{10,1... | collective-permute-start | bytes 589832 | tf_op jit(solution)/shard_map/ppermute | solution.py:19
  35.6 8.4 %collective-permute-start.3 = (bf16[96,1024]{1,0:T(8,128)(2,1)S(1)}, bf16[96,1024]{1,0:T(8,128)(2,1)S(1)}, u32[]{:S(2)}, u32[]{:S(2)}) collective-permute-start(bf16[96,1024]{1,0:T(8,128)(2,1)S(1)} %collective-permute-done.2), channel_id=1, source_target_pairs={{0,1},{1,2},{2,3},{3,4},{4,5},{5,6},{6,7},{7,0},{8,9},{9,10},{10,1... | collective-permute-start | bytes 589832 | tf_op jit(solution)/shard_map/ppermute | solution.py:19
  43.9 8.4 %collective-permute-start.4 = (bf16[96,1024]{1,0:T(8,128)(2,1)S(1)}, bf16[96,1024]{1,0:T(8,128)(2,1)S(1)}, u32[]{:S(2)}, u32[]{:S(2)}) collective-permute-start(bf16[96,1024]{1,0:T(8,128)(2,1)S(1)} %collective-permute-done.3), channel_id=1, source_target_pairs={{0,1},{1,2},{2,3},{3,4},{4,5},{5,6},{6,7},{7,0},{8,9},{9,10},{10,1... | collective-permute-start | bytes 589832 | tf_op jit(solution)/shard_map/ppermute | solution.py:19
  52.3 9.3 %collective-permute-start.5 = (bf16[96,1024]{1,0:T(8,128)(2,1)S(1)}, bf16[96,1024]{1,0:T(8,128)(2,1)S(1)}, u32[]{:S(2)}, u32[]{:S(2)}) collective-permute-start(bf16[96,1024]{1,0:T(8,128)(2,1)S(1)} %collective-permute-done.4), channel_id=1, source_target_pairs={{0,1},{1,2},{2,3},{3,4},{4,5},{5,6},{6,7},{7,0},{8,9},{9,10},{10,1... | collective-permute-start | bytes 589832 | tf_op jit(solution)/shard_map/ppermute | solution.py:19
  61.6 8.4 %collective-permute-start.6 = (bf16[96,1024]{1,0:T(8,128)(2,1)S(1)}, bf16[96,1024]{1,0:T(8,128)(2,1)S(1)}, u32[]{:S(2)}, u32[]{:S(2)}) collective-permute-start(bf16[96,1024]{1,0:T(8,128)(2,1)S(1)} %collective-permute-done.5), channel_id=1, source_target_pairs={{0,1},{1,2},{2,3},{3,4},{4,5},{5,6},{6,7},{7,0},{8,9},{9,10},{10,1... | collective-permute-start | bytes 589832 | tf_op jit(solution)/shard_map/ppermute | solution.py:19
  71.1 1.5 copy-start.2
  72.5 244.2 %reduce-scatter.3.cloned.1.call-start = ((), (), s32[]{:S(2)}) async-start(), calls=%async_computation.3 | async-start | bytes 15728640 | tf_op jit(solution)/shard_map/reduce_scatter | solution.py:49
  72.6 91.0 %copy-start.1 = (s32[384]{0:T(512)S(1)}, s32[384]{0:T(512)}, u32[]{:S(2)}) copy-start(s32[384]{0:T(512)} %param.6) | copy-start | bytes 4612
  216.9 179.0 %reduce-scatter.5.cloned.1.call-start = ((), (), s32[]{:S(2)}) async-start(), calls=%async_computation.4 | async-start | bytes 3538944 | tf_op jit(solution)/shard_map/reduce_scatter | solution.py:57
Sparse Core Ops, SparseCore 0:
  72.6 43.5 all-gather.1
  217.1 99.6 reduce-scatter.2
  320.9 74.9 reduce-scatter.4
